TPU v7x, 512 devices: a whole 4x4x16 slice. The times are simulated.
512 devices in a mesh: dom: 64 (over x, z_lo, core), feat: 8 (over z_hi, y).
Axes of the slice: x: 4, y: 4, z: 16 (z_hi: 2, z_lo: 8; z = z_hi * 8 + z_lo), core: 2. Of those that a mesh axis runs over, the one named last changes fastest.
Arguments:
- fine_latent: bfloat16 [256, 1048576], P('feat', 'dom'), may hold values from -6 to 6
- coarse_latent: bfloat16 [256, 524288], P('feat', 'dom'), may hold values from -6 to 6
- parents: int32 [4, 1048576], P(None, 'dom'), may hold values from 0 to 24575, as said below
- interp_weights: float32 [4, 1048576], P(None, 'dom'), may hold values from 0.1 to 1
- live_rows: int32 [64], P('dom'), may hold values from 8192 to 16384, as said below
- w_fine: bfloat16 [256, 256], replicated, may hold values from -0.25 to 0.25
- w_parent: bfloat16 [256, 256], replicated, may hold values from -0.25 to 0.25
- w_edge_out: bfloat16 [256, 256], replicated, may hold values from -0.375 to 0.375
- w_node_fine: bfloat16 [256, 256], replicated, may hold values from -0.25 to 0.25
- w_node_agg: bfloat16 [256, 256], replicated, may hold values from -0.25 to 0.25
- w_node_out: bfloat16 [256, 256], replicated, may hold values from -0.375 to 0.375
- edge_bias: float32 [256], replicated, may hold values from -3 to 3
- node_bias: float32 [256], replicated, may hold values from -3 to 3
- norm_gain: float32 [256], replicated, may hold values from 0.1 to 1.9
- norm_bias: float32 [256], replicated, may hold values from -2 to 2
Outputs:
- fine_out: bfloat16 [256, 1048576], P('feat', 'dom')
Inputs may be any that keep to these rules, and one draw needn't show every extreme that they name: `parents`: a parent slot s of a fine node of block b names coarse node (b - 1) * 8192 + s, block b holding coarse nodes b * 8192 to (b + 1) * 8192 - 1; slots of block 0 are at least 8192, slots of the last block under 2 * 8192. `live_rows`: fine node slots of a block at or beyond its count are padding; at least one block is full.
All inputs are finite; a program needn't handle non-finite values.
Results may differ from a plain program's by a relative error of at most 0.0042.
Values may be sent and summed in bfloat16 or wider, within the bound.
A program may use at most 128 MiB of HBM per device.

v0:
```python
import jax
import jax.numpy as jnp
from jax import lax
from jax.sharding import PartitionSpec as P


def padded(block, sides, width):
    for axis, dim in sides:
        count = lax.axis_size(axis)
        forward = [(i, i + 1) for i in range(count - 1)]
        backward = [(target, source) for source, target in forward]
        low = lax.ppermute(
            lax.slice_in_dim(block, block.shape[dim] - width, None, axis=dim), axis, forward
        )
        high = lax.ppermute(lax.slice_in_dim(block, 0, width, axis=dim), axis, backward)
        block = jnp.concatenate([low, block, high], axis=dim)
    return block


def update(latent, parent_rows, weights, params):
    (
        w_fine,
        w_edge_out,
        w_node_fine,
        w_node_agg,
        w_node_out,
        edge_bias,
        node_bias,
        norm_gain,
        norm_bias,
    ) = params
    fine_part = jnp.dot(latent, w_fine, preferred_element_type=jnp.float32) + edge_bias
    edge_hidden = jnp.maximum(fine_part[None] + parent_rows.astype(jnp.float32), 0.0).astype(
        jnp.bfloat16
    )
    width = edge_hidden.shape[2]
    message = jnp.dot(
        edge_hidden.reshape(-1, width), w_edge_out, preferred_element_type=jnp.float32
    ).reshape(edge_hidden.shape)
    aggregate = jnp.sum(weights[:, :, None] * message, axis=0).astype(jnp.bfloat16)
    node_pre = (
        jnp.dot(latent, w_node_fine, preferred_element_type=jnp.float32)
        + jnp.dot(aggregate, w_node_agg, preferred_element_type=jnp.float32)
        + node_bias
    )
    node_hidden = jnp.maximum(node_pre, 0.0).astype(jnp.bfloat16)
    output = jnp.dot(node_hidden, w_node_out, preferred_element_type=jnp.float32)
    centre = jnp.mean(output, axis=-1, keepdims=True)
    centered = output - centre
    spread = jnp.mean(centered * centered, axis=-1, keepdims=True)
    normed = centered * lax.rsqrt(spread + 1e-05) * norm_gain + norm_bias
    return (latent.astype(jnp.float32) + normed).astype(jnp.bfloat16)


def project_columns(columns, weight):
    return lax.dot_general(
        columns, weight, (((0,), (0,)), ((), ())), preferred_element_type=jnp.float32
    ).astype(jnp.bfloat16)


def shards(
    fine_latent,
    coarse_latent,
    parents,
    interp_weights,
    live_rows,
    w_fine,
    w_parent,
    w_edge_out,
    w_node_fine,
    w_node_agg,
    w_node_out,
    edge_bias,
    node_bias,
    norm_gain,
    norm_bias,
):
    params = (
        w_fine,
        w_edge_out,
        w_node_fine,
        w_node_agg,
        w_node_out,
        edge_bias,
        node_bias,
        norm_gain,
        norm_bias,
    )
    groups = lax.axis_size("feat")
    feat_rank = lax.axis_index("feat")
    coarse_rows = coarse_latent.shape[1]
    fine_count = fine_latent.shape[1]
    per_device = fine_count // groups
    own_rows = lax.all_to_all(fine_latent, "feat", split_axis=1, concat_axis=0, tiled=True).T
    positions = feat_rank * per_device + jnp.arange(per_device, dtype=jnp.int32)
    my_parents = lax.dynamic_slice_in_dim(parents, feat_rank * per_device, per_device, 1)
    my_weights = lax.dynamic_slice_in_dim(interp_weights, feat_rank * per_device, per_device, 1)
    projected = None
    full_width = lax.all_gather(coarse_latent, "feat", axis=0, tiled=True)
    framed = padded(full_width, (("dom", 1),), coarse_rows)
    projected = project_columns(framed, w_parent)
    live_count = live_rows[0]
    active = jnp.sum((positions < live_count).astype(jnp.int32))
    block_rows = min(512, per_device)
    steps_needed = (active + block_rows - 1) // block_rows

    def one_step(number, current):
        first_row = number * block_rows
        latent = lax.dynamic_slice_in_dim(own_rows, first_row, block_rows, 0)
        weights = lax.dynamic_slice_in_dim(my_weights, first_row, block_rows, 1)
        slot_block = lax.dynamic_slice_in_dim(my_parents, first_row, block_rows, 1)
        parent_rows = jnp.take(projected, slot_block, axis=0)
        updated = update(latent, parent_rows, weights, params)
        keep_rows = lax.dynamic_slice_in_dim(positions, first_row, block_rows, 0) < live_count
        updated = jnp.where(keep_rows[:, None], updated, latent)
        return lax.dynamic_update_slice_in_dim(current, updated, first_row, 0)

    result = lax.fori_loop(0, steps_needed, one_step, own_rows)
    fine_out = lax.all_to_all(result.T, "feat", split_axis=0, concat_axis=1, tiled=True)
    return fine_out


def solution(mesh):
    in_specs = (
        P("feat", "dom"),
        P("feat", "dom"),
        P(None, "dom"),
        P(None, "dom"),
        P("dom"),
        P(),
        P(),
        P(),
        P(),
        P(),
        P(),
        P(),
        P(),
        P(),
        P(),
    )
    out_specs = P("feat", "dom")
    return jax.shard_map(shards, mesh=mesh, in_specs=in_specs, out_specs=out_specs, check_vma=False)
```

profile of v0, /device:TPU:37, one launch (start us, length us, event | category | flops | bytes accessed | tf_op | source)
XLA Modules:
  0.0 494.1 jit_solution(10758784765913863180)
XLA Ops:
  7.3 172.0 %all-gather.2.cloned.1.call-done = bf16[256,8192]{1,0:T(8,128)(2,1)} async-done(((bf16[32,8192]{1,0:T(8,128)(2,1)}), bf16[256,8192]{1,0:T(8,128)(2,1)}) %all-gather.2.cloned.1.call-update) | async-done | bytes 4194320 | tf_op jit(solution)/shard_map/all_gather | solution.py:99
  179.2 11.7 %collective-permute-start = (bf16[256,8192]{1,0:T(8,128)(2,1)}, bf16[256,8192]{1,0:T(8,128)(2,1)}, u32[]{:S(2)}, u32[]{:S(2)}) collective-permute-start(bf16[256,8192]{1,0:T(8,128)(2,1)} %all-gather.2.cloned.1.call-done), channel_id=1, source_target_pairs={{0,8},{8,16},{16,24},{24,32},{32,40},{40,48},{48,56},{56,64},{64,7... | collective-permute-start | bytes 12582920 | tf_op jit(solution)/shard_map/ppermute | solution.py:12
  191.0 1.9 collective-permute-start.1
  192.9 2.3 copy.25
  195.2 4.3 all-to-all-start
  202.1 1.4 constant_dynamic-slice_fusion.2
  203.4 33.7 %all-to-all-done = bf16[32,8,2048]{2,0,1:T(8,128)(2,1)S(1)} async-done(((bf16[32,8,2048]{2,0,1:T(8,128)(2,1)}), bf16[32,8,2048]{2,0,1:T(8,128)(2,1)S(1)}, u32[]{:S(2)}, u32[]{:S(2)}) %all-to-all-start) | async-done | bytes 1048608 | tf_op jit(solution)/shard_map/all_to_all | solution.py:94
  237.2 1.0 copy.30
  238.2 43.5 %collective-permute-done = bf16[256,8192]{1,0:T(8,128)(2,1)} collective-permute-done((bf16[256,8192]{1,0:T(8,128)(2,1)}, bf16[256,8192]{1,0:T(8,128)(2,1)}, u32[]{:S(2)}, u32[]{:S(2)}) %collective-permute-start) | collective-permute-done | bytes 4194336 | tf_op jit(solution)/shard_map/ppermute | solution.py:12
  281.7 13.1 %collective-permute-done.1 = bf16[256,8192]{1,0:T(8,128)(2,1)} collective-permute-done((bf16[256,8192]{1,0:T(8,128)(2,1)}, bf16[256,8192]{1,0:T(8,128)(2,1)}, u32[]{:S(2)}, u32[]{:S(2)}) %collective-permute-start.1) | collective-permute-done | bytes 4194336 | tf_op jit(solution)/shard_map/ppermute | solution.py:15
  294.8 15.1 %convolution_convert_fusion = bf16[24576,256]{1,0:T(8,128)(2,1)} fusion(bf16[256,256]{1,0:T(8,128)(2,1)S(1)} %copy-done.6, bf16[256,8192]{1,0:T(8,128)(2,1)} %collective-permute-done.1, bf16[256,8192]{1,0:T(8,128)(2,1)} %all-gather.2.cloned.1.call-done, bf16[256,8192]{1,0:T(8,128)(2,1)} %collective-permute-done), kind=kOutput, calls=%fused_computation.38 | convolution fusion | flops 3265265664 | bytes 25296896 | tf_op jit(solution)/shard_map/dot_general | solution.py:56
  309.9 84.5 %while.10 = (s32[]{:T(128)}, bf16[2048,256]{0,1:T(8,128)(2,1)}, s32[]{:T(128)}, s32[2048]{0:T(1024)S(1)}, s32[]{:T(128)}, /*index=5*/bf16[2048,256]{0,1:T(8,128)...) while((s32[]{:T(128)}, bf16[2048,256]{0,1:T(8,128)(2,1)}, ...), condition=%wide.region_5.6_spmd, body=%wide.region_1.5_spmd.sunk | while | flops 542659584 | bytes 9164051 | solution.py:118
  309.9 1.0 convolution_add_fusion.3
  311.6 12.8 %gather_fusion = bf16[2048,256]{1,0:T(8,128)(2,1)S(1)} fusion(bf16[24576,256]{1,0:T(8,128)(2,1)} %get-tuple-element.306, s32[2048]{0:T(1024)S(1)} %broadcast_clamp_fusion.2), kind=kCustom, calls=%fused_computation.clone.1 | custom fusion | bytes 2105344 | tf_op jit(solution)/shard_map/while/body/jit(_take)/gather | solution.py:112
  325.9 1.8 multiply_reduce_fusion.4
  327.9 1.4 fusion.60
  331.0 0.9 convolution_add_fusion.3
  332.7 12.8 %gather_fusion = bf16[2048,256]{1,0:T(8,128)(2,1)S(1)} fusion(bf16[24576,256]{1,0:T(8,128)(2,1)} %get-tuple-element.306, s32[2048]{0:T(1024)S(1)} %broadcast_clamp_fusion.2), kind=kCustom, calls=%fused_computation.clone.1 | custom fusion | bytes 2105344 | tf_op jit(solution)/shard_map/while/body/jit(_take)/gather | solution.py:112
  347.0 1.8 multiply_reduce_fusion.4
  349.0 1.4 fusion.60
  351.2 0.9 fusion.61
  352.1 0.9 convolution_add_fusion.3
  353.8 12.8 %gather_fusion = bf16[2048,256]{1,0:T(8,128)(2,1)S(1)} fusion(bf16[24576,256]{1,0:T(8,128)(2,1)} %get-tuple-element.306, s32[2048]{0:T(1024)S(1)} %broadcast_clamp_fusion.2), kind=kCustom, calls=%fused_computation.clone.1 | custom fusion | bytes 2105344 | tf_op jit(solution)/shard_map/while/body/jit(_take)/gather | solution.py:112
  368.1 1.8 multiply_reduce_fusion.4
  370.1 1.4 fusion.60
  373.2 0.9 convolution_add_fusion.3
  374.9 12.8 %gather_fusion = bf16[2048,256]{1,0:T(8,128)(2,1)S(1)} fusion(bf16[24576,256]{1,0:T(8,128)(2,1)} %get-tuple-element.306, s32[2048]{0:T(1024)S(1)} %broadcast_clamp_fusion.2), kind=kCustom, calls=%fused_computation.clone.1 | custom fusion | bytes 2105344 | tf_op jit(solution)/shard_map/while/body/jit(_take)/gather | solution.py:112
  389.2 1.8 multiply_reduce_fusion.4
  391.2 1.4 fusion.60
  393.4 0.9 fusion.61
  394.4 91.9 %all_to_all.38 = bf16[8,32,2048]{2,1,0:T(8,128)(2,1)S(1)} all-to-all(bf16[8,32,2048]{2,1,0:T(8,128)(2,1)} %bitcast.51), channel_id=1, replica_groups=mesh['dom'=64,'feat'=8] {'feat'}, dimensions={0} | all-to-all | bytes 2097152 | tf_op jit(solution)/shard_map/all_to_all | solution.py:119
  486.2 1.1 copy.23
  (61 shorter events, 16.8 us)
Async XLA Ops:
  6.5 194.9 %copy-start = (s32[4,16384]{1,0:T(4,128)S(1)}, s32[4,16384]{1,0:T(4,128)}, u32[]{:S(2)}) copy-start(s32[4,16384]{1,0:T(4,128)} %param.19) | copy-start | bytes 786436
  6.5 288.2 %copy-start.6 = (bf16[256,256]{1,0:T(8,128)(2,1)S(1)}, bf16[256,256]{1,0:T(8,128)(2,1)}, u32[]{:S(2)}) copy-start(bf16[256,256]{1,0:T(8,128)(2,1)} %param.23) | copy-start | bytes 393220
  6.5 172.7 %all-gather.2.cloned.1.call-start = ((), (), s32[]{:S(2)}) async-start(), calls=%async_computation.2 | async-start | bytes 4718592 | tf_op jit(solution)/shard_map/all_gather | solution.py:99
  179.2 102.5 %collective-permute-start = (bf16[256,8192]{1,0:T(8,128)(2,1)}, bf16[256,8192]{1,0:T(8,128)(2,1)}, u32[]{:S(2)}, u32[]{:S(2)}) collective-permute-start(bf16[256,8192]{1,0:T(8,128)(2,1)} %all-gather.2.cloned.1.call-done), channel_id=1, source_target_pairs={{0,8},{8,16},{16,24},{24,32},{32,40},{40,48},{48,56},{56,64},{64,7... | collective-permute-start | bytes 12582920 | tf_op jit(solution)/shard_map/ppermute | solution.py:12
  191.0 103.8 %collective-permute-start.1 = (bf16[256,8192]{1,0:T(8,128)(2,1)}, bf16[256,8192]{1,0:T(8,128)(2,1)}, u32[]{:S(2)}, u32[]{:S(2)}) collective-permute-start(bf16[256,8192]{1,0:T(8,128)(2,1)} %all-gather.2.cloned.1.call-done), channel_id=1, source_target_pairs={{8,0},{16,8},{24,16},{32,24},{40,32},{48,40},{56,48},{64,56},{72,6... | collective-permute-start | bytes 12582920 | tf_op jit(solution)/shard_map/ppermute | solution.py:15
  195.2 41.9 %all-to-all-start = ((bf16[32,8,2048]{2,0,1:T(8,128)(2,1)}), bf16[32,8,2048]{2,0,1:T(8,128)(2,1)S(1)}, u32[]{:S(2)}, u32[]{:S(2)}) async-start(bf16[32,8,2048]{2,0,1:T(8,128)(2,1)} %bitcast.28), calls=%async_computation | async-start | bytes 2097152 | tf_op jit(solution)/shard_map/all_to_all | solution.py:94
  238.1 71.7 %copy-start.1 = (bf16[256,256]{1,0:T(8,128)(2,1)S(1)}, bf16[256,256]{1,0:T(8,128)(2,1)}, u32[]{:S(2)}) copy-start(bf16[256,256]{1,0:T(8,128)(2,1)} %param.25) | copy-start | bytes 393220
  238.1 71.7 %copy-start.2 = (bf16[256,256]{1,0:T(8,128)(2,1)S(1)}, bf16[256,256]{1,0:T(8,128)(2,1)}, u32[]{:S(2)}) copy-start(bf16[256,256]{1,0:T(8,128)(2,1)} %param.22) | copy-start | bytes 393220
  238.1 71.7 %copy-start.3 = (bf16[256,256]{1,0:T(8,128)(2,1)S(1)}, bf16[256,256]{1,0:T(8,128)(2,1)}, u32[]{:S(2)}) copy-start(bf16[256,256]{1,0:T(8,128)(2,1)} %param.26) | copy-start | bytes 393220
  238.1 71.7 %copy-start.4 = (f32[256]{0:T(256)S(1)}, f32[256]{0:T(256)}, u32[]{:S(2)}) copy-start(f32[256]{0:T(256)} %param.30) | copy-start | bytes 3076
  238.1 71.7 %copy-start.5 = (f32[256]{0:T(256)S(1)}, f32[256]{0:T(256)}, u32[]{:S(2)}) copy-start(f32[256]{0:T(256)} %param.31) | copy-start | bytes 3076
Sparse Core Ops, SparseCore 0:
  10.5 168.6 all-gather.1
where the time goes:
time: 495 us; the launch traced here: 494 us
  waiting for transfers between devices  263 us (53%)
  blocking collectives  91.9 us (19%)
  local copies, waits for them, and re-layouts  60.5 us (12%)
  matrix products  32.6 us (7%)
  starting transfers between devices  18 us (4%)
  between operations  14.7 us (3%)
  other arithmetic  13.3 us (3%)
    all_gather x1, waiting for transfers between devices, shards(): full_width = lax.all_gather(coarse_latent, 'feat', axis=0, tiled=True)  172 us
    all_to_all x1, blocking collectives, shards(): lax.all_to_all(result.T, 'feat', split_axis=0, concat_axis=1, tiled=True)  91.9 us
    gather x4, local copies, waits for them, and re-layouts, one_step(): parent_rows = jnp.take(projected, slot_block, axis=0)  51.3 us
    ppermute x1, waiting for transfers between devices, padded(): lax.ppermute(lax.slice_in_dim(block, block.shape[dim] - width, None, axis...  43.5 us
    all_to_all x1, waiting for transfers between devices, shards(): lax.all_to_all(fine_latent, 'feat', split_axis=1, concat_axis=0, tiled=True)  33.7 us
    dot_general x1, matrix products, project_columns(): lax.dot_general(columns, weight, (((0,), (0,)), ((), ())), preferred_elem...  15.1 us
    ppermute x1, waiting for transfers between devices, padded(): lax.ppermute(lax.slice_in_dim(block, 0, width, axis=dim), axis, backward)  13.1 us
    ppermute x1, starting transfers between devices, padded(): lax.ppermute(lax.slice_in_dim(block, block.shape[dim] - width, None, axis...  11.7 us
  transfers between devices with their start and end apart: 4, of which 4 were waited for; matrix products, arithmetic and copies ran while one was open for 1% of the time, Pallas kernels for 0%

commit v1 on v0

v1 whole, which is shorter than its diff:
```python
import jax
import jax.numpy as jnp
from jax import lax
from jax.experimental import pallas as pl
from jax.experimental.pallas import tpu as pltpu
from jax.sharding import PartitionSpec as P

MESH = pl.DeviceIdType.MESH
ANY = pl.BlockSpec(memory_space=pl.ANY)
VMEM = pl.BlockSpec(memory_space=pltpu.VMEM)
SMEM = pl.BlockSpec(memory_space=pltpu.SMEM)
DMA = pltpu.SemaphoreType.DMA
VMEM_LIMIT = 60 * 1024 * 1024

D = 256
HALF = 128
FEAT = 8
RING = 4
DOM = 64
SLICE = D // FEAT
PARTS = 4
PEERS = ((1, 0), (1, 1), (1, 3), (1, 2), (0, 1), (0, 3), (0, 2))
F32 = jnp.float32
BF16 = jnp.bfloat16


def dot(a, b, da, db):
    return lax.dot_general(a, b, (((da,), (db,)), ((), ())), preferred_element_type=F32)


def place():
    dom = lax.axis_index("dom")
    feat = lax.axis_index("feat")
    half = feat // RING
    ring = lax.rem(feat, RING)
    core = lax.rem(dom, 2)
    return dom, feat, half, ring, core


def feat_of(half, ring, a, b):
    return lax.rem(half + a, 2) * RING + lax.rem(ring + b, RING)


def seam_neighbour(dom, feat, core):
    target = lax.rem(dom + DOM + 2 * core - 1, DOM)
    low = lax.rem(dom // 2, 8)
    edge = jnp.where(core == 1, low == 7, low == 0)
    return target, jnp.where(edge, lax.rem(feat + RING, FEAT), feat)


def remote(src, dst, send, recv, device):
    return pltpu.make_async_remote_copy(
        src_ref=src, dst_ref=dst, send_sem=send, recv_sem=recv, device_id=device, device_id_type=MESH
    )


def collect_kernel(
    coarse, fine, w_parent, table, fine_full,
    landed, rows, c_s, c_r, f_s, f_r, n_s, n_r, p_s, p_r, z_s, z_r, local,
):
    dom, feat, half, ring, core = place()
    block = coarse.shape[1]
    share = block // RING
    part = share // PARTS
    mine = fine_full.shape[1]
    partner = (dom + 1 - 2 * core, feat)
    outer = seam_neighbour(dom, feat, core)
    up = (dom, feat_of(half, ring, 0, 1))
    down = (dom, feat_of(half, ring, 0, 3))
    own_base = block
    pair_base = core * 2 * block
    outer_base = (1 - core) * 2 * block
    edge_base = core * 2 * block

    barrier = pltpu.get_barrier_semaphore()
    friends = [(dom, feat_of(half, ring, a, b)) for a, b in PEERS] + [partner, outer]
    for friend in friends:
        pl.semaphore_signal(barrier, inc=1, device_id=friend, device_id_type=MESH)
    pl.semaphore_wait(barrier, len(friends))

    def aligned(x, m):
        return pl.multiple_of(x, m)

    def table_part(base, owner, q):
        return table.at[pl.ds(aligned(base + owner * share + q * part, part), part)]

    sends = []

    def go(copy):
        copy.start()
        sends.append(copy)

    my_rows = pl.ds(aligned(feat * SLICE, SLICE), SLICE)

    def coarse_out(q):
        for i, (a, b) in enumerate(PEERS):
            to = lax.rem(ring + b, RING)
            go(remote(
                coarse.at[:, pl.ds(aligned(to * share + q * part, part), part)],
                landed.at[my_rows, pl.ds(q * part, part)],
                c_s.at[i, q], c_r.at[i, q], (dom, feat_of(half, ring, a, b)),
            ))

    def coarse_in(q):
        for i in range(len(PEERS)):
            ref = landed.at[pl.ds(0, SLICE), pl.ds(q * part, part)]
            remote(ref, ref, c_s.at[i, q], c_r.at[i, q], partner).wait_recv()

    def fine_out(i):
        a, b = PEERS[i]
        to = feat_of(half, ring, a, b)
        go(remote(
            fine.at[:, pl.ds(aligned(to * mine, mine), mine)],
            fine_full.at[my_rows, :],
            f_s.at[i], f_r.at[i], (dom, to),
        ))

    def arrived(ref, recv, send):
        remote(ref, ref, send, recv, partner).wait_recv()

    def spread(kind, base, q):
        src = rows.at[pl.ds(q * part, part)] if kind == 0 else table_part(base, ring, q)
        go(remote(src, table_part(base, ring, q), n_s.at[kind, 0, q], n_r.at[kind, 0, q], up))
        go(remote(src, table_part(base, ring, q), n_s.at[kind, 1, q], n_r.at[kind, 1, q], down))

    def pass_on(kind, base, q):
        below = lax.rem(ring + 3, RING)
        above = lax.rem(ring + 1, RING)
        arrived(table_part(base, below, q), n_r.at[kind, 0, q], n_s.at[kind, 0, q])
        if q % 2 == 0:
            ref = table_part(base, below, q)
            go(remote(ref, ref, n_s.at[kind, 2, q], n_r.at[kind, 2, q], up))
        arrived(table_part(base, above, q), n_r.at[kind, 1, q], n_s.at[kind, 1, q])
        if q % 2 == 1:
            ref = table_part(base, above, q)
            go(remote(ref, ref, n_s.at[kind, 2, q], n_r.at[kind, 2, q], down))
        if kind == 0:
            to_pair(below, q, 1)
            to_pair(above, q, 2)

    def far_in(kind, base, q):
        far = lax.rem(ring + 2, RING)
        arrived(table_part(base, far, q), n_r.at[kind, 2, q], n_s.at[kind, 2, q])
        if kind == 0:
            to_pair(far, q, 3)

    def to_pair(owner, q, i):
        src = rows.at[pl.ds(q * part, part)] if i == 0 else table_part(own_base, owner, q)
        go(remote(src, table_part(pair_base, owner, q), p_s.at[i, q], p_r.at[i, q], partner))

    keep_coarse = pltpu.make_async_copy(
        coarse.at[:, pl.ds(aligned(ring * share, share), share)], landed.at[my_rows, :], local.at[0]
    )
    keep_coarse.start()
    coarse_out(0)
    coarse_out(1)
    keep_fine = pltpu.make_async_copy(
        fine.at[:, pl.ds(aligned(feat * mine, mine), mine)], fine_full.at[my_rows, :], local.at[1]
    )
    keep_fine.start()
    keep_coarse.wait()
    keeps = [keep_fine]

    def project(q):
        coarse_in(q)
        columns = pl.ds(q * part, part)
        product = dot(landed[:, columns], w_parent[...], 0, 0).astype(BF16)
        rows[columns, :, :] = product.reshape(part, 2, HALF)
        spread(0, own_base, q)
        to_pair(ring, q, 0)
        go(remote(
            rows.at[columns], table_part(outer_base, ring, q), z_s.at[q], z_r.at[q], outer
        ))
        keep = pltpu.make_async_copy(rows.at[columns], table_part(own_base, ring, q), local.at[2 + q])
        keep.start()
        keeps.append(keep)

    def relay(q):
        pass_on(0, own_base, q)
        arrived(table_part(edge_base, ring, q), z_r.at[q], z_s.at[q])
        spread(1, edge_base, q)

    def relay_edge(q):
        far_in(0, own_base, q)
        pass_on(1, edge_base, q)

    for q in range(PARTS + 2):
        if q < PARTS:
            project(q)
            if q + 2 < PARTS:
                coarse_out(q + 2)
            if q == PARTS - 2:
                for i in range(4):
                    fine_out(i)
            if q == PARTS - 1:
                for i in range(4, 7):
                    fine_out(i)
        if 1 <= q <= PARTS:
            relay(q - 1)
        if q >= 2:
            relay_edge(q - 2)
    other_base = (1 - core) * 2 * block
    for q in range(PARTS):
        far_in(1, edge_base, q)
        for i in range(4):
            ref = table_part(other_base, i, q)
            arrived(ref, p_r.at[i, q], p_s.at[i, q])
    for i in range(len(PEERS)):
        ref = fine_full.at[pl.ds(0, SLICE), :]
        arrived(ref, f_r.at[i], f_s.at[i])
    for keep in keeps:
        keep.wait()
    for copy in sends:
        copy.wait_send()


def collect(coarse, fine, w_parent):
    block = coarse.shape[1]
    share = block // RING
    mine = fine.shape[1] // FEAT
    return pl.pallas_call(
        collect_kernel,
        out_shape=(
            jax.ShapeDtypeStruct((3 * block, 2, HALF), BF16),
            jax.ShapeDtypeStruct((D, mine), BF16),
        ),
        in_specs=[ANY, ANY, VMEM],
        out_specs=(ANY, ANY),
        scratch_shapes=[
            pltpu.VMEM((D, share), BF16),
            pltpu.VMEM((share, 2, HALF), BF16),
            DMA((7, PARTS)), DMA((7, PARTS)),
            DMA((7,)), DMA((7,)),
            DMA((2, 3, PARTS)), DMA((2, 3, PARTS)),
            DMA((4, PARTS)), DMA((4, PARTS)),
            DMA((PARTS,)), DMA((PARTS,)),
            DMA((2 + PARTS,)),
        ],
        compiler_params=pltpu.CompilerParams(
            collective_id=0, has_side_effects=True, vmem_limit_bytes=VMEM_LIMIT
        ),
    )(coarse, fine, w_parent)


def column(ref):
    return jnp.transpose(jnp.broadcast_to(ref[...], (8, D)))[:, 0:1]


STEP = 512
UNROLL = 8


def nodes_kernel(
    parents, weights, live, table, fine, w_fine, w_edge_out, w_node_fine, w_node_agg, w_node_out,
    edge_bias, node_bias, norm_gain, norm_bias, out,
    near, pre, hidden, sem,
):
    load = pltpu.make_async_copy(table, near, sem)
    load.start()
    mine = fine.shape[1]
    first = lax.axis_index("feat") * mine
    node_col, gain_col, bias_col = column(node_bias), column(norm_gain), column(norm_bias)

    for step in range(mine // STEP):
        latent = fine[:, step * STEP:(step + 1) * STEP]
        fine_part = dot(latent, w_fine[...], 0, 0) + edge_bias[...]
        pre[...] = fine_part.reshape(STEP, 2, HALF)
        if step == 0:
            load.wait()

        def gather(j, carry):
            for u in range(UNROLL):
                i = j * UNROLL + u
                own = pre[i]
                total = None
                for k in range(PARENTS):
                    slot = parents[k, step * STEP + i]
                    value = jnp.maximum(own + near[slot].astype(F32), 0.0)
                    value = value.astype(BF16).astype(F32) * weights[k, step * STEP + i]
                    total = value if total is None else total + value
                hidden[i] = total
            return carry

        lax.fori_loop(0, STEP // UNROLL, gather, 0)
        mixed = hidden[...].reshape(STEP, D).astype(BF16)
        aggregate = dot(w_edge_out[...], mixed, 0, 1).astype(BF16)
        node_pre = dot(w_node_fine[...], latent, 0, 0) + dot(w_node_agg[...], aggregate, 0, 0) + node_col
        node_hidden = jnp.maximum(node_pre, 0.0).astype(BF16)
        update = dot(w_node_out[...], node_hidden, 0, 0)
        centre = jnp.mean(update, axis=0, keepdims=True)
        centered = update - centre
        spread = jnp.mean(centered * centered, axis=0, keepdims=True)
        normed = centered * lax.rsqrt(spread + 1e-05) * gain_col + bias_col
        updated = (latent.astype(F32) + normed).astype(BF16)
        position = first + step * STEP + lax.broadcasted_iota(jnp.int32, (1, STEP), 1)
        out[:, step * STEP:(step + 1) * STEP] = jnp.where(position < live[0], updated, latent)


PARENTS = 4


def nodes(parents, weights, live, table, fine, *params):
    mine = fine.shape[1]
    return pl.pallas_call(
        nodes_kernel,
        out_shape=jax.ShapeDtypeStruct((D, mine), BF16),
        in_specs=[SMEM, SMEM, SMEM, ANY] + [VMEM] * 10,
        out_specs=VMEM,
        scratch_shapes=[
            pltpu.VMEM(table.shape, BF16),
            pltpu.VMEM((STEP, 2, HALF), F32),
            pltpu.VMEM((STEP, 2, HALF), F32),
            DMA,
        ],
        compiler_params=pltpu.CompilerParams(vmem_limit_bytes=VMEM_LIMIT),
    )(parents, weights, live, table, fine, *params)


def deliver_kernel(result, out, send, recv, local):
    dom, feat, half, ring, core = place()
    mine = result.shape[1]
    barrier = pltpu.get_barrier_semaphore()
    for a, b in PEERS:
        pl.semaphore_signal(
            barrier, inc=1, device_id=(dom, feat_of(half, ring, a, b)), device_id_type=MESH
        )
    pl.semaphore_wait(barrier, len(PEERS))
    here = out.at[:, pl.ds(pl.multiple_of(feat * mine, mine), mine)]
    copies = []
    for i, (a, b) in enumerate(PEERS):
        to = feat_of(half, ring, a, b)
        copy = remote(
            result.at[pl.ds(pl.multiple_of(to * SLICE, SLICE), SLICE), :], here,
            send.at[i], recv.at[i], (dom, to),
        )
        copy.start()
        copies.append(copy)
    keep = pltpu.make_async_copy(
        result.at[pl.ds(pl.multiple_of(feat * SLICE, SLICE), SLICE), :], here, local
    )
    keep.start()
    keep.wait()
    for copy in copies:
        copy.wait()


def deliver(result, fine_count):
    return pl.pallas_call(
        deliver_kernel,
        out_shape=jax.ShapeDtypeStruct((SLICE, fine_count), BF16),
        in_specs=[ANY],
        out_specs=ANY,
        scratch_shapes=[DMA((7,)), DMA((7,)), DMA],
        compiler_params=pltpu.CompilerParams(collective_id=1, has_side_effects=True),
    )(result)


def shards(
    fine_latent, coarse_latent, parents, interp_weights, live_rows, w_fine, w_parent, w_edge_out,
    w_node_fine, w_node_agg, w_node_out, edge_bias, node_bias, norm_gain, norm_bias,
):
    mine = fine_latent.shape[1] // FEAT
    first = lax.axis_index("feat") * mine
    my_parents = lax.dynamic_slice_in_dim(parents, first, mine, 1)
    my_weights = lax.dynamic_slice_in_dim(interp_weights, first, mine, 1)
    table, fine = collect(coarse_latent, fine_latent, w_parent)
    result = nodes(
        my_parents, my_weights, live_rows, table, fine, w_fine, w_edge_out, w_node_fine,
        w_node_agg, w_node_out, edge_bias[None], node_bias[None], norm_gain[None], norm_bias[None],
    )
    return deliver(result, fine_latent.shape[1])


def solution(mesh):
    in_specs = (
        P("feat", "dom"), P("feat", "dom"), P(None, "dom"), P(None, "dom"), P("dom"),
        P(), P(), P(), P(), P(), P(), P(), P(), P(), P(),
    )
    return jax.shard_map(
        shards, mesh=mesh, in_specs=in_specs, out_specs=P("feat", "dom"), check_vma=False
    )
```

time: 495 us -> 225 us (0.45)
  the two profiles are of different devices: /device:TPU:37 before, /device:TPU:1 now
where the time goes in v1:
time: 225 us; the launch traced here: 224 us
  Pallas kernels  219 us (97%)
  local copies, waits for them, and re-layouts  4.51 us (2%)
    pallas_call x1, Pallas kernels, collect(): pl.pallas_call(collect_kernel, out_shape=(jax.ShapeDtypeStruct((3 * block...  138 us
    pallas_call x1, Pallas kernels, deliver(): pl.pallas_call(deliver_kernel, out_shape=jax.ShapeDtypeStruct((SLICE, fin...  54.9 us
    pallas_call x1, Pallas kernels, nodes(): pl.pallas_call(nodes_kernel, out_shape=jax.ShapeDtypeStruct((D, mine), BF...  26.7 us

profile of v1, /device:TPU:1, one launch (start us, length us, event | category | flops | bytes accessed | tf_op | source)
XLA Modules:
  0.0 224.5 jit_solution(1942464152706799603)
XLA Ops:
  0.0 0.0 copy-start
  0.7 0.3 copy-done
  1.0 0.6 constant_dynamic-slice_fusion.1.parents
  1.6 1.4 constant_dynamic-slice_fusion.weights
  2.9 137.7 %shard_map.145 = (bf16[24576,2,128]{2,1,0:T(2,128)(2,1)}, bf16[256,2048]{1,0:T(8,128)(2,1)}) custom-call(bf16[32,8192]{1,0:T(8,128)(2,1)} %coarse.1, bf16[32,16384]{1,0:T(8,128)(2,1)} %fine.1, bf16[256,256]{1,0:T(8,128)(2,1)} %w_parent.1), custom_call_target="tpu_custom_call" | custom-call | tf_op jit(solution)/shard_map/pallas_call | solution.py:221
  140.6 26.7 %shard_map.146.result = bf16[256,2048]{1,0:T(8,128)(2,1)} custom-call(s32[4,2048]{1,0:T(4,128)} %constant_dynamic-slice_fusion.1.parents, f32[4,2048]{1,0:T(4,128)} %constant_dynamic-slice_fusion.weights, s32[1]{0:T(128)S(6)} %copy.17.live, bf16[24576,2,128]{2,1,0:T(2,128)(2,1)} %get-tuple-element.7.table, bf16[256,2048]{1,0:T(8,128)(2,1)} %get-tuple-element.8.fine, ...), custom_call_target="tpu_custom_call" | custom-call | tf_op jit(solution)/shard_map/pallas_call | solution.py:304
  167.3 54.9 %shard_map.147 = bf16[32,16384]{1,0:T(8,128)(2,1)} custom-call(bf16[256,2048]{1,0:T(8,128)(2,1)} %shard_map.146.result), custom_call_target="tpu_custom_call" | custom-call | tf_op jit(solution)/shard_map/pallas_call | solution.py:348
  222.2 2.3 %copy.18 = bf16[32,16384]{1,0:T(8,128)(2,1)} copy(bf16[32,16384]{1,0:T(8,128)(2,1)} %shard_map.147) | data formatting | bytes 2097152
Async XLA Ops:
  0.0 1.0 copy-start

commit v2 on v1

v2 whole, which is shorter than its diff:
```python
import jax
import jax.numpy as jnp
from jax import lax
from jax.experimental import pallas as pl
from jax.experimental.pallas import tpu as pltpu
from jax.sharding import PartitionSpec as P

MESH = pl.DeviceIdType.MESH
ANY = pl.BlockSpec(memory_space=pl.ANY)
VMEM = pl.BlockSpec(memory_space=pltpu.VMEM)
SMEM = pl.BlockSpec(memory_space=pltpu.SMEM)
DMA = pltpu.SemaphoreType.DMA
VMEM_LIMIT = 60 * 1024 * 1024

D = 256
HALF = 128
FEAT = 8
RING = 4
DOM = 64
SLICE = D // FEAT
PARTS = 4
PARENTS = 4
STEP = 512
UNROLL = 8
PEERS = ((1, 0), (1, 1), (1, 3), (1, 2), (0, 1), (0, 3), (0, 2))
F32 = jnp.float32
BF16 = jnp.bfloat16


def dot(a, b, da, db):
    return lax.dot_general(a, b, (((da,), (db,)), ((), ())), preferred_element_type=F32)


def place():
    dom = lax.axis_index("dom")
    feat = lax.axis_index("feat")
    half = feat // RING
    ring = lax.rem(feat, RING)
    core = lax.rem(dom, 2)
    return dom, feat, half, ring, core


def feat_of(half, ring, a, b):
    return lax.rem(half + a, 2) * RING + lax.rem(ring + b, RING)


def seam_neighbour(dom, feat, core):
    target = lax.rem(dom + DOM + 2 * core - 1, DOM)
    low = lax.rem(dom // 2, 8)
    edge = jnp.where(core == 1, low == 7, low == 0)
    return target, jnp.where(edge, lax.rem(feat + RING, FEAT), feat)


def remote(src, dst, send, recv, device):
    return pltpu.make_async_remote_copy(
        src_ref=src, dst_ref=dst, send_sem=send, recv_sem=recv, device_id=device, device_id_type=MESH
    )


def column(ref):
    return jnp.transpose(jnp.broadcast_to(ref[...], (8, D)))[:, 0:1]


def kernel(
    coarse, fine, parents, weights, live, w_parent, w_fine, w_edge_out, w_node_fine, w_node_agg,
    w_node_out, edge_bias, node_bias, norm_gain, norm_bias, out,
    landed, near, latents, result, pre, hidden, slots, scales,
    c_s, c_r, f_s, f_r, n_s, n_r, p_s, p_r, z_s, z_r, o_s, o_r, local, kept,
):
    dom, feat, half, ring, core = place()
    block = coarse.shape[1]
    share = block // RING
    part = share // PARTS
    mine = latents.shape[1]
    steps = mine // STEP
    partner = (dom + 1 - 2 * core, feat)
    outer = seam_neighbour(dom, feat, core)
    up = (dom, feat_of(half, ring, 0, 1))
    down = (dom, feat_of(half, ring, 0, 3))
    own_base = block
    edge_base = core * 2 * block
    other_base = (1 - core) * 2 * block

    def aligned(start, size):
        return pl.ds(pl.multiple_of(start, size), size)

    my_rows = aligned(feat * SLICE, SLICE)
    table_loads = (
        pltpu.make_async_copy(parents.at[:, aligned(feat * mine, mine)], slots, local.at[0]),
        pltpu.make_async_copy(weights.at[:, aligned(feat * mine, mine)], scales, local.at[1]),
        pltpu.make_async_copy(coarse.at[:, aligned(ring * share, share)], landed.at[my_rows, :], local.at[2]),
        pltpu.make_async_copy(fine.at[:, aligned(feat * mine, mine)], latents.at[my_rows, :], local.at[3]),
    )
    for load in table_loads:
        load.start()

    barrier = pltpu.get_barrier_semaphore()
    friends = [(dom, feat_of(half, ring, a, b)) for a, b in PEERS] + [partner, outer]
    for friend in friends:
        pl.semaphore_signal(barrier, inc=1, device_id=friend, device_id_type=MESH)
    pl.semaphore_wait(barrier, len(friends))

    def rows_of(base, owner, q):
        return near.at[aligned(base + owner * share + q * part, part)]

    sends = []

    def go(copy):
        copy.start()
        sends.append(copy)

    def arrived(ref, recv, send):
        remote(ref, ref, send, recv, partner).wait_recv()

    def coarse_out(q):
        for i, (a, b) in enumerate(PEERS):
            to = lax.rem(ring + b, RING)
            go(remote(
                coarse.at[:, aligned(to * share + q * part, part)],
                landed.at[my_rows, pl.ds(q * part, part)],
                c_s.at[i, q], c_r.at[i, q], (dom, feat_of(half, ring, a, b)),
            ))

    def coarse_in(q):
        for i in range(len(PEERS)):
            arrived(landed.at[pl.ds(0, SLICE), pl.ds(q * part, part)], c_r.at[i, q], c_s.at[i, q])

    def fine_out(j):
        for i, (a, b) in enumerate(PEERS):
            to = feat_of(half, ring, a, b)
            go(remote(
                fine.at[:, aligned(to * mine + j * STEP, STEP)],
                latents.at[my_rows, pl.ds(j * STEP, STEP)],
                f_s.at[i, j], f_r.at[i, j], (dom, to),
            ))

    def spread(kind, base, q):
        ref = rows_of(base, ring, q)
        go(remote(ref, ref, n_s.at[kind, 0, q], n_r.at[kind, 0, q], up))
        go(remote(ref, ref, n_s.at[kind, 1, q], n_r.at[kind, 1, q], down))

    def to_pair(owner, q, i):
        go(remote(
            rows_of(own_base, owner, q), rows_of(edge_base, owner, q), p_s.at[i, q], p_r.at[i, q], partner
        ))

    def pass_on(kind, base, q):
        below = lax.rem(ring + 3, RING)
        above = lax.rem(ring + 1, RING)
        ref = rows_of(base, below, q)
        arrived(ref, n_r.at[kind, 0, q], n_s.at[kind, 0, q])
        if q % 2 == 0:
            go(remote(ref, ref, n_s.at[kind, 2, q], n_r.at[kind, 2, q], up))
        ref = rows_of(base, above, q)
        arrived(ref, n_r.at[kind, 1, q], n_s.at[kind, 1, q])
        if q % 2 == 1:
            go(remote(ref, ref, n_s.at[kind, 2, q], n_r.at[kind, 2, q], down))
        if kind == 0:
            to_pair(below, q, 1)
            to_pair(above, q, 2)

    def far_in(kind, base, q):
        far = lax.rem(ring + 2, RING)
        arrived(rows_of(base, far, q), n_r.at[kind, 2, q], n_s.at[kind, 2, q])
        if kind == 0:
            to_pair(far, q, 3)

    def project(q):
        coarse_in(q)
        product = dot(landed[:, q * part:(q + 1) * part], w_parent[...], 0, 0).astype(BF16)
        near[aligned(own_base + ring * share + q * part, part), :, :] = product.reshape(part, 2, HALF)
        spread(0, own_base, q)
        ref = rows_of(own_base, ring, q)
        go(remote(ref, rows_of(other_base, ring, q), z_s.at[q], z_r.at[q], outer))
        to_pair(ring, q, 0)

    def relay(q):
        pass_on(0, own_base, q)
        arrived(rows_of(edge_base, ring, q), z_r.at[q], z_s.at[q])
        spread(1, edge_base, q)

    def relay_edge(q):
        far_in(0, own_base, q)
        pass_on(1, edge_base, q)

    coarse_out(0)
    coarse_out(1)
    for load in table_loads:
        load.wait()
    for q in range(PARTS + 2):
        if q < PARTS:
            project(q)
            if q + 2 < PARTS:
                coarse_out(q + 2)
        if 2 <= q:
            for j in range((q - 2) * steps // PARTS, (q - 1) * steps // PARTS):
                fine_out(j)
        if 1 <= q <= PARTS:
            relay(q - 1)
        if 2 <= q:
            relay_edge(q - 2)
    for q in range(PARTS):
        far_in(1, edge_base, q)
        for i in range(4):
            arrived(rows_of(other_base, i, q), p_r.at[i, q], p_s.at[i, q])

    node_col, gain_col, bias_col = column(node_bias), column(norm_gain), column(norm_bias)
    here = feat * mine

    def deliver(j, i):
        a, b = PEERS[i]
        to = feat_of(half, ring, a, b)
        return remote(
            result.at[aligned(to * SLICE, SLICE), aligned(j * STEP, STEP)],
            out.at[:, aligned(here + j * STEP, STEP)],
            o_s.at[i, j], o_r.at[i, j], (dom, to),
        )

    def keep(j):
        return pltpu.make_async_copy(
            result.at[my_rows, aligned(j * STEP, STEP)], out.at[:, aligned(here + j * STEP, STEP)], kept.at[j]
        )

    def step(j, carry):
        columns = aligned(j * STEP, STEP)
        for i in range(len(PEERS)):
            arrived(latents.at[pl.ds(0, SLICE), columns], f_r.at[i, j], f_s.at[i, j])
        latent = latents[:, columns]
        fine_part = dot(latent, w_fine[...], 0, 0) + edge_bias[...]
        pre[...] = fine_part.reshape(STEP, 2, HALF)

        def gather(n, carry):
            for u in range(UNROLL):
                i = n * UNROLL + u
                own = pre[i]
                total = None
                for k in range(PARENTS):
                    value = jnp.maximum(own + near[slots[k, j * STEP + i]].astype(F32), 0.0)
                    value = value.astype(BF16).astype(F32) * scales[k, j * STEP + i]
                    total = value if total is None else total + value
                hidden[i] = total
            return carry

        lax.fori_loop(0, STEP // UNROLL, gather, 0)
        mixed = hidden[...].reshape(STEP, D).astype(BF16)
        aggregate = dot(w_edge_out[...], mixed, 0, 1).astype(BF16)
        node_pre = dot(w_node_fine[...], latent, 0, 0) + dot(w_node_agg[...], aggregate, 0, 0) + node_col
        node_hidden = jnp.maximum(node_pre, 0.0).astype(BF16)
        update = dot(w_node_out[...], node_hidden, 0, 0)
        centre = jnp.mean(update, axis=0, keepdims=True)
        centered = update - centre
        spread_out = jnp.mean(centered * centered, axis=0, keepdims=True)
        normed = centered * lax.rsqrt(spread_out + 1e-05) * gain_col + bias_col
        updated = (latent.astype(F32) + normed).astype(BF16)
        position = here + j * STEP + lax.broadcasted_iota(jnp.int32, (1, STEP), 1)
        result[:, columns] = jnp.where(position < live[0], updated, latent)
        for i in range(len(PEERS)):
            deliver(j, i).start()
        keep(j).start()
        return carry

    lax.fori_loop(0, steps, step, 0)
    for copy in sends:
        copy.wait_send()

    def finish(j, carry):
        keep(j).wait()
        for i in range(len(PEERS)):
            deliver(j, i).wait()
        return carry

    lax.fori_loop(0, steps, finish, 0)


def shards(
    fine_latent, coarse_latent, parents, interp_weights, live_rows, w_fine, w_parent, w_edge_out,
    w_node_fine, w_node_agg, w_node_out, edge_bias, node_bias, norm_gain, norm_bias,
):
    fine_count = fine_latent.shape[1]
    block = coarse_latent.shape[1]
    mine = fine_count // FEAT
    steps = mine // STEP
    return pl.pallas_call(
        kernel,
        out_shape=jax.ShapeDtypeStruct((SLICE, fine_count), BF16),
        in_specs=[ANY, ANY, ANY, ANY, SMEM] + [VMEM] * 10,
        out_specs=ANY,
        scratch_shapes=[
            pltpu.VMEM((D, block // RING), BF16),
            pltpu.VMEM((3 * block, 2, HALF), BF16),
            pltpu.VMEM((D, mine), BF16),
            pltpu.VMEM((D, mine), BF16),
            pltpu.VMEM((STEP, 2, HALF), F32),
            pltpu.VMEM((STEP, 2, HALF), F32),
            pltpu.SMEM((PARENTS, mine), jnp.int32),
            pltpu.SMEM((PARENTS, mine), F32),
            DMA((7, PARTS)), DMA((7, PARTS)),
            DMA((7, steps)), DMA((7, steps)),
            DMA((2, 3, PARTS)), DMA((2, 3, PARTS)),
            DMA((4, PARTS)), DMA((4, PARTS)),
            DMA((PARTS,)), DMA((PARTS,)),
            DMA((7, steps)), DMA((7, steps)),
            DMA((4,)), DMA((steps,)),
        ],
        compiler_params=pltpu.CompilerParams(
            collective_id=0, has_side_effects=True, vmem_limit_bytes=VMEM_LIMIT
        ),
    )(
        coarse_latent, fine_latent, parents, interp_weights, live_rows, w_parent, w_fine, w_edge_out,
        w_node_fine, w_node_agg, w_node_out, edge_bias[None], node_bias[None], norm_gain[None],
        norm_bias[None],
    )


def solution(mesh):
    in_specs = (
        P("feat", "dom"), P("feat", "dom"), P(None, "dom"), P(None, "dom"), P("dom"),
        P(), P(), P(), P(), P(), P(), P(), P(), P(), P(),
    )
    return jax.shard_map(
        shards, mesh=mesh, in_specs=in_specs, out_specs=P("feat", "dom"), check_vma=False
    )
```

time: 225 us -> 188 us (0.84)
  the two profiles are of different devices: /device:TPU:1 before, /device:TPU:38 now
where the time goes in v2:
time: 188 us
  Pallas kernels  185 us (98%)
  local copies, waits for them, and re-layouts  2.26 us (1%)
    pallas_call x1, Pallas kernels, shards(): pl.pallas_call(kernel, out_shape=jax.ShapeDtypeStruct((SLICE, fine_count)...  185 us

profile of v2, /device:TPU:38, one launch (start us, length us, event | category | flops | bytes accessed | tf_op | source)
XLA Modules:
  0.0 188.0 jit_solution(9679623446964767395)
XLA Ops:
  0.7 185.0 %shard_map.145 = bf16[32,16384]{1,0:T(8,128)(2,1)} custom-call(bf16[32,8192]{1,0:T(8,128)(2,1)} %coarse.1, bf16[32,16384]{1,0:T(8,128)(2,1)} %fine.1, s32[4,16384]{1,0:T(4,128)} %parents.1, f32[4,16384]{1,0:T(4,128)} %weights.1, s32[1]{0:T(128)S(6)} %copy.17.live, bf16[256,256]{1,0:T(8,128)(2,1)} %w_parent.1, bf16[256,256]{1,0:T(8,128)(2,1)} %w_fine.1, ...), custom_call_target="tpu_custom_call" | custom-call | tf_op jit(solution)/shard_map/pallas_call | solution.py:283
  185.7 2.3 %copy.18 = bf16[32,16384]{1,0:T(8,128)(2,1)} copy(bf16[32,16384]{1,0:T(8,128)(2,1)} %shard_map.145) | data formatting | bytes 2097152

commit v3 on v2

v3 whole, which is shorter than its diff:
```python
import jax
import jax.numpy as jnp
from jax import lax
from jax.experimental import pallas as pl
from jax.experimental.pallas import tpu as pltpu
from jax.sharding import PartitionSpec as P

MESH = pl.DeviceIdType.MESH
ANY = pl.BlockSpec(memory_space=pl.ANY)
VMEM = pl.BlockSpec(memory_space=pltpu.VMEM)
DMA = pltpu.SemaphoreType.DMA
VMEM_LIMIT = 60 * 1024 * 1024

D = 256
HALF = 128
FEAT = 8
RING = 4
SLICE = D // FEAT
PARTS = 4
PARENTS = 4
OWNERS = 8
STEP = 512
UNROLL = 8
F32 = jnp.float32
BF16 = jnp.bfloat16


def dot(a, b, da, db):
    return lax.dot_general(a, b, (((da,), (db,)), ((), ())), preferred_element_type=F32)


def remote(src, dst, send, recv, device):
    return pltpu.make_async_remote_copy(
        src_ref=src, dst_ref=dst, send_sem=send, recv_sem=recv, device_id=device, device_id_type=MESH
    )


def column(ref):
    return jnp.transpose(jnp.broadcast_to(ref[...], (8, D)))[:, 0:1]


def device(x, y, z, core):
    return x * 16 + lax.rem(z, 8) * 2 + core, (z // 8) * RING + y


def kernel(
    coarse, fine, parents, weights, w_parent, w_fine, w_edge_out, w_node_fine, w_node_agg,
    w_node_out, edge_bias, node_bias, norm_gain, norm_bias, out, slots_in, scales_in,
    coarse_held, fine_held, landed, near, latents, result, back, pre, hidden,
    slots, scales,
    hc_s, hc_r, hf_s, hf_r, c_s, c_r, f_s, f_r, n_s, n_r, p_s, p_r, e_s, e_r,
    a_s, a_r, b_s, b_r, o_s, o_r, w_s, w_r, local,
):
    dom = lax.axis_index("dom")
    feat = lax.axis_index("feat")
    x, j_own, core = dom // 16, lax.rem(dom // 2, 8), lax.rem(dom, 2)
    half, y = feat // RING, lax.rem(feat, RING)
    z = half * 8 + j_own
    kind_x = lax.rem(x, 2)
    base_x = x - kind_x
    owner = y * 2 + core
    swapped = kind_x != core
    block = coarse.shape[1]
    part = block // OWNERS // PARTS
    group = OWNERS * part
    mine = latents.shape[1]
    steps = mine // STEP
    wide = OWNERS * STEP

    def aligned(start, size):
        return pl.ds(pl.multiple_of(start, size), size)

    work_z = lax.rem(j_own + 8 * core + 4, 16)
    from_u = lax.rem(z + 12, 16)
    from_j, from_core = lax.rem(from_u, 8), from_u // 8

    def worker(y_to, core_to):
        return device(x, y_to, work_z, core_to)

    def holder(y_to, half_to):
        return device(x, y_to, from_j + 8 * half_to, from_core)

    twin = device(base_x + 1 - kind_x, y, z, 1 - core)
    partner = device(x, y, z, 1 - core)
    up = device(x, lax.rem(y + 1, RING), z, core)
    down = device(x, lax.rem(y + 3, RING), z, core)
    flat = device(base_x + 1 - kind_x, y, z, core)
    turn = jnp.where(kind_x == 0, z == 4, z == 3)
    inside = base_x + 1 - kind_x
    across = lax.rem(x + 3 + 2 * kind_x, 4)
    slant = device(
        jnp.where(turn, across, inside), y, lax.rem(z + 15 + 2 * kind_x, 16), core
    )
    edges_to = device(base_x + core, y, lax.rem(j_own + 8 * kind_x + 4, 16), half)
    edges_from = device(base_x + from_core, y, from_j + 8 * core, kind_x)

    barrier = pltpu.get_barrier_semaphore()
    friends = [worker(lax.rem(y + b, RING), e) for b in range(RING) for e in range(2)]
    friends += [holder(lax.rem(y + b, RING), e) for b in range(RING) for e in range(2)]
    friends += [twin, partner, up, down, flat, slant, edges_to, edges_from]
    for friend in friends:
        pl.semaphore_signal(barrier, inc=1, device_id=friend, device_id_type=MESH)
    pl.semaphore_wait(barrier, len(friends))

    center_base = block
    flat_base = (1 - kind_x) * 2 * block
    slant_base = kind_x * 2 * block
    bases = (center_base, flat_base, slant_base)

    sends = []

    def go(copy):
        copy.start()
        sends.append(copy)

    def arrived(ref, recv, send):
        remote(ref, ref, send, recv, partner).wait_recv()

    def rows_of(base, who, q):
        return near.at[aligned(base + q * group + who * part, part)]

    def hold(src, dst, send, recv, kept, starting):
        there = remote(src, dst, send, recv, twin)
        here = pltpu.make_async_copy(src, dst, kept)

        @pl.when(swapped)
        def _():
            if starting:
                there.start()
            else:
                there.wait()

        @pl.when(jnp.logical_not(swapped))
        def _():
            if starting:
                here.start()
            else:
                here.wait()

    def hold_coarse(q, starting):
        columns = pl.ds(q * group, group)
        hold(coarse.at[:, columns], coarse_held.at[:, columns], hc_s.at[q], hc_r.at[q], local.at[q], starting)

    def hold_fine(j, starting):
        columns = pl.ds(j * wide, wide)
        hold(fine.at[:, columns], fine_held.at[:, columns], hf_s.at[j], hf_r.at[j], local.at[PARTS + j], starting)

    my_rows = aligned(feat * SLICE, SLICE)

    def coarse_out(q):
        hold_coarse(q, False)
        for b in range(RING):
            for e in range(2):
                to = lax.rem(y + b, RING)
                go(remote(
                    coarse_held.at[:, aligned(q * group + (to * 2 + e) * part, part)],
                    landed.at[my_rows, pl.ds(q * part, part)],
                    c_s.at[b * 2 + e, q], c_r.at[feat, q], worker(to, e),
                ))

    def fine_out(j):
        hold_fine(j, False)
        for b in range(RING):
            for e in range(2):
                to = lax.rem(y + b, RING)
                go(remote(
                    fine_held.at[:, aligned(j * wide + (to * 2 + e) * STEP, STEP)],
                    latents.at[my_rows, pl.ds(j * STEP, STEP)],
                    f_s.at[b * 2 + e, j], f_r.at[feat, j], worker(to, e),
                ))

    def edges_out():
        for j in range(steps):
            columns = aligned(j * wide + (y * 2 + half) * STEP, STEP)
            place = pl.ds(j * STEP, STEP)
            go(remote(parents.at[:, columns], slots_in.at[:, place], a_s.at[j], a_r.at[j], edges_to))
            go(remote(weights.at[:, columns], scales_in.at[:, place], b_s.at[j], b_r.at[j], edges_to))

    def edges_in():
        for j in range(steps):
            place = pl.ds(j * STEP, STEP)
            arrived(slots_in.at[:, place], a_r.at[j], a_s.at[j])
            arrived(scales_in.at[:, place], b_r.at[j], b_s.at[j])
        moves = (
            pltpu.make_async_copy(slots_in, slots, local.at[PARTS + steps]),
            pltpu.make_async_copy(scales_in, scales, local.at[PARTS + steps + 1]),
        )
        for move in moves:
            move.start()
        for move in moves:
            move.wait()

    def to_pair(kind, ring, i, q):
        ref = rows_of(bases[kind], ring * 2 + core, q)
        go(remote(ref, ref, p_s.at[kind, i, q], p_r.at[kind, i, q], partner))

    def spread(kind, q):
        ref = rows_of(bases[kind], owner, q)
        go(remote(ref, ref, n_s.at[kind, 0, q], n_r.at[kind, 0, q], up))
        go(remote(ref, ref, n_s.at[kind, 1, q], n_r.at[kind, 1, q], down))
        to_pair(kind, y, 0, q)

    def pass_on(kind, q):
        below, above = lax.rem(y + 3, RING), lax.rem(y + 1, RING)
        ref = rows_of(bases[kind], below * 2 + core, q)
        arrived(ref, n_r.at[kind, 0, q], n_s.at[kind, 0, q])
        if q % 2 == 0:
            go(remote(ref, ref, n_s.at[kind, 2, q], n_r.at[kind, 2, q], up))
        ref = rows_of(bases[kind], above * 2 + core, q)
        arrived(ref, n_r.at[kind, 1, q], n_s.at[kind, 1, q])
        if q % 2 == 1:
            go(remote(ref, ref, n_s.at[kind, 2, q], n_r.at[kind, 2, q], down))
        to_pair(kind, below, 1, q)
        to_pair(kind, above, 2, q)

    def far_in(kind, q):
        far = lax.rem(y + 2, RING)
        arrived(rows_of(bases[kind], far * 2 + core, q), n_r.at[kind, 2, q], n_s.at[kind, 2, q])
        to_pair(kind, far, 3, q)

    def project(q):
        for s in range(OWNERS):
            arrived(landed.at[pl.ds(0, SLICE), pl.ds(q * part, part)], c_r.at[s, q], c_s.at[s, q])
        product = dot(landed[:, q * part:(q + 1) * part], w_parent[...], 0, 0).astype(BF16)
        near[aligned(center_base + q * group + owner * part, part), :, :] = product.reshape(part, 2, HALF)
        ref = rows_of(center_base, owner, q)
        go(remote(ref, rows_of(slant_there, owner, q), e_s.at[1, q], e_r.at[1, q], slant))
        go(remote(ref, rows_of(flat_there, owner, q), e_s.at[0, q], e_r.at[0, q], flat))
        spread(0, q)

    flat_there = kind_x * 2 * block
    slant_there = (1 - kind_x) * 2 * block

    def relay(q):
        pass_on(0, q)
        for kind in (1, 2):
            arrived(rows_of(bases[kind], owner, q), e_r.at[kind - 1, q], e_s.at[kind - 1, q])
            spread(kind, q)

    def relay_edge(q):
        far_in(0, q)
        pass_on(1, q)
        pass_on(2, q)

    for q in range(PARTS):
        hold_coarse(q, True)
    hold_fine(0, True)
    coarse_out(0)
    coarse_out(1)
    for q in range(PARTS + 2):
        if q < PARTS:
            project(q)
            if q + 2 < PARTS:
                coarse_out(q + 2)
        if q + 1 < steps:
            hold_fine(q + 1, True)
        if q == 1:
            edges_out()
        if 2 <= q < 2 + steps:
            fine_out(q - 2)
        if 1 <= q <= PARTS:
            relay(q - 1)
        if 2 <= q:
            relay_edge(q - 2)
    for kind in (1, 2):
        for q in range(PARTS):
            far_in(kind, q)
    edges_in()
    for kind in range(3):
        for q in range(PARTS):
            for i in range(4):
                arrived(rows_of(bases[kind], i * 2 + 1 - core, q), p_r.at[kind, i, q], p_s.at[kind, i, q])

    node_col, gain_col, bias_col = column(node_bias), column(norm_gain), column(norm_bias)

    def deliver(j, b, e):
        to = lax.rem(y + b, RING)
        return remote(
            result.at[aligned((e * RING + to) * SLICE, SLICE), aligned(j * STEP, STEP)],
            back.at[:, aligned(j * wide + owner * STEP, STEP)],
            o_s.at[b * 2 + e, j], o_r.at[owner, j], holder(to, e),
        )

    def hand_back(j, starting):
        columns = aligned(j * wide, wide)
        hold(back.at[:, columns], out.at[:, columns], w_s.at[j], w_r.at[j], local.at[j], starting)

    def returned(j):
        for s in range(OWNERS):
            arrived(back.at[:, aligned(j * wide, STEP)], o_r.at[s, j], o_s.at[s, j])
        hand_back(j, True)

    def step(j, carry):
        columns = aligned(j * STEP, STEP)
        for s in range(OWNERS):
            arrived(latents.at[pl.ds(0, SLICE), columns], f_r.at[s, j], f_s.at[s, j])
        latent = latents[:, columns]
        fine_part = dot(latent, w_fine[...], 0, 0) + edge_bias[...]
        pre[...] = fine_part.reshape(STEP, 2, HALF)

        def gather(n, carry):
            for u in range(UNROLL):
                i = n * UNROLL + u
                own = pre[i]
                total = None
                for k in range(PARENTS):
                    value = jnp.maximum(own + near[slots[k, j * STEP + i]].astype(F32), 0.0)
                    value = value.astype(BF16).astype(F32) * scales[k, j * STEP + i]
                    total = value if total is None else total + value
                hidden[i] = total
            return carry

        lax.fori_loop(0, STEP // UNROLL, gather, 0)
        mixed = hidden[...].reshape(STEP, D).astype(BF16)
        aggregate = dot(w_edge_out[...], mixed, 0, 1).astype(BF16)
        node_pre = dot(w_node_fine[...], latent, 0, 0) + dot(w_node_agg[...], aggregate, 0, 0) + node_col
        node_hidden = jnp.maximum(node_pre, 0.0).astype(BF16)
        update = dot(w_node_out[...], node_hidden, 0, 0)
        centre = jnp.mean(update, axis=0, keepdims=True)
        centered = update - centre
        variance = jnp.mean(centered * centered, axis=0, keepdims=True)
        normed = centered * lax.rsqrt(variance + 1e-05) * gain_col + bias_col
        result[:, columns] = (latent.astype(F32) + normed).astype(BF16)
        for b in range(RING):
            for e in range(2):
                deliver(j, b, e).start()

        @pl.when(j > 0)
        def _():
            returned(j - 1)

        return carry

    lax.fori_loop(0, steps, step, 0)
    returned(steps - 1)
    for copy in sends:
        copy.wait_send()

    def finish(j, carry):
        hand_back(j, False)
        for b in range(RING):
            for e in range(2):
                deliver(j, b, e).wait_send()
        return carry

    lax.fori_loop(0, steps, finish, 0)


def shards(
    fine_latent, coarse_latent, parents, interp_weights, live_rows, w_fine, w_parent, w_edge_out,
    w_node_fine, w_node_agg, w_node_out, edge_bias, node_bias, norm_gain, norm_bias,
):
    fine_count = fine_latent.shape[1]
    block = coarse_latent.shape[1]
    mine = fine_count // OWNERS
    steps = mine // STEP
    pairs = [
        (PARTS,), (steps,), (OWNERS, PARTS), (OWNERS, steps), (3, 3, PARTS), (3, 4, PARTS),
        (2, PARTS), (steps,), (steps,), (OWNERS, steps), (steps,),
    ]
    updated, _, _ = pl.pallas_call(
        kernel,
        out_shape=(
            jax.ShapeDtypeStruct((SLICE, fine_count), BF16),
            jax.ShapeDtypeStruct((PARENTS, mine), jnp.int32),
            jax.ShapeDtypeStruct((PARENTS, mine), F32),
        ),
        in_specs=[ANY] * 4 + [VMEM] * 10,
        out_specs=(ANY, ANY, ANY),
        scratch_shapes=[
            pltpu.VMEM((SLICE, block), BF16),
            pltpu.VMEM((SLICE, fine_count), BF16),
            pltpu.VMEM((D, block // OWNERS), BF16),
            pltpu.VMEM((3 * block, 2, HALF), BF16),
            pltpu.VMEM((D, mine), BF16),
            pltpu.VMEM((D, mine), BF16),
            pltpu.VMEM((SLICE, fine_count), BF16),
            pltpu.VMEM((STEP, 2, HALF), F32),
            pltpu.VMEM((STEP, 2, HALF), F32),
            pltpu.SMEM((PARENTS, mine), jnp.int32),
            pltpu.SMEM((PARENTS, mine), F32),
        ] + [DMA(shape) for shape in pairs for _ in range(2)] + [DMA((PARTS + steps + 2,))],
        compiler_params=pltpu.CompilerParams(
            collective_id=0, has_side_effects=True, vmem_limit_bytes=VMEM_LIMIT
        ),
    )(
        coarse_latent, fine_latent, parents, interp_weights, w_parent, w_fine, w_edge_out,
        w_node_fine, w_node_agg, w_node_out, edge_bias[None], node_bias[None], norm_gain[None],
        norm_bias[None],
    )
    live = jnp.arange(fine_count, dtype=jnp.int32) < live_rows[0]
    return jnp.where(live[None, :], updated, fine_latent)


def solution(mesh):
    in_specs = (
        P("feat", "dom"), P("feat", "dom"), P(None, "dom"), P(None, "dom"), P("dom"),
        P(), P(), P(), P(), P(), P(), P(), P(), P(), P(),
    )
    return jax.shard_map(
        shards, mesh=mesh, in_specs=in_specs, out_specs=P("feat", "dom"), check_vma=False
    )
```

time: 188 us -> 176 us (0.936)
  the two profiles are of different devices: /device:TPU:38 before, /device:TPU:6 now
where the time goes in v3:
time: 176 us
  Pallas kernels  173 us (98%)
  other arithmetic  2.42 us (1%)
    pallas_call x1, Pallas kernels, shards(): pl.pallas_call(kernel, out_shape=(jax.ShapeDtypeStruct((SLICE, fine_count...  173 us

profile of v3, /device:TPU:6, one launch (start us, length us, event | category | flops | bytes accessed | tf_op | source)
XLA Modules:
  0.0 176.0 jit_solution(3897672154306985904)
XLA Ops:
  0.7 0.0 copy-start
  0.7 172.9 %shard_map.145 = (bf16[32,16384]{1,0:T(8,128)(2,1)}, s32[4,2048]{1,0:T(4,128)}, f32[4,2048]{1,0:T(4,128)}) custom-call(bf16[32,8192]{1,0:T(8,128)(2,1)} %coarse.1, bf16[32,16384]{1,0:T(8,128)(2,1)} %fine.1, s32[4,16384]{1,0:T(4,128)} %parents.1, f32[4,16384]{1,0:T(4,128)} %weights.1, bf16[256,256]{1,0:T(8,128)(2,1)} %w_parent.1, bf16[256,256]{1,0:T(8,128)(2,1)} %w_fine.1, ...), custom_call_target="tpu_custom_call" | custom-call | tf_op jit(solution)/shard_map/pallas_call | solution.py:361
  173.6 0.0 copy-done
  173.6 2.4 %broadcast_select_fusion = bf16[32,16384]{1,0:T(8,128)(2,1)} fusion(bf16[32,16384]{1,0:T(8,128)(2,1)} %get-tuple-element.6, bf16[32,16384]{1,0:T(8,128)(2,1)S(1)} %copy-done, pred[16384]{0:T(1024)(128)(4,1)S(1)} %iota_compare_fusion), kind=kLoop, calls=%fused_computation | loop fusion | flops 524288 | bytes 3162112 | tf_op jit(solution)/shard_map/jit(_where)/select_n | solution.py:392
  (1 shorter events, 0.0 us)
Async XLA Ops:
  0.7 172.9 %copy-start = (bf16[32,16384]{1,0:T(8,128)(2,1)S(1)}, bf16[32,16384]{1,0:T(8,128)(2,1)}, u32[]{:S(2)}) copy-start(bf16[32,16384]{1,0:T(8,128)(2,1)} %fine.1) | copy-start | bytes 3145732

commit v4 on v3

--- a/solution.py
+++ b/solution.py
@@ -244,7 +244,8 @@
 
     for q in range(PARTS):
         hold_coarse(q, True)
-    hold_fine(0, True)
+    for j in range(steps // PARTS):
+        hold_fine(j, True)
     coarse_out(0)
     coarse_out(1)
     for q in range(PARTS + 2):
@@ -252,16 +253,18 @@
             project(q)
             if q + 2 < PARTS:
                 coarse_out(q + 2)
-        if q + 1 < steps:
-            hold_fine(q + 1, True)
+        if q + 1 < PARTS:
+            for j in range((q + 1) * steps // PARTS, (q + 2) * steps // PARTS):
+                hold_fine(j, True)
         if q == 1:
             edges_out()
-        if 2 <= q < 2 + steps:
-            fine_out(q - 2)
         if 1 <= q <= PARTS:
             relay(q - 1)
         if 2 <= q:
             relay_edge(q - 2)
+        if 2 <= q:
+            for j in range((q - 2) * steps // PARTS, (q - 1) * steps // PARTS):
+                fine_out(j)
     for kind in (1, 2):
         for q in range(PARTS):
             far_in(kind, q)
@@ -283,7 +286,7 @@
 
     def hand_back(j, starting):
         columns = aligned(j * wide, wide)
-        hold(back.at[:, columns], out.at[:, columns], w_s.at[j], w_r.at[j], local.at[j], starting)
+        hold(back.at[:, columns], out.at[:, columns], w_s.at[j], w_r.at[j], local.at[PARTS + j], starting)
 
     def returned(j):
         for s in range(OWNERS):

time: 176 us -> 170 us (0.966)
  the two profiles are of different devices: /device:TPU:6 before, /device:TPU:1 now
where the time goes in v4:
time: 170 us; the launch traced here: 169 us
  Pallas kernels  166 us (98%)
  other arithmetic  2.42 us (1%)
    pallas_call x1, Pallas kernels, shards(): pl.pallas_call(kernel, out_shape=(jax.ShapeDtypeStruct((SLICE, fine_count...  166 us

profile of v4, /device:TPU:1, one launch (start us, length us, event | category | flops | bytes accessed | tf_op | source)
XLA Modules:
  0.0 168.8 jit_solution(3408342751357395640)
XLA Ops:
  0.7 0.0 copy-start
  0.7 165.7 %shard_map.145 = (bf16[32,16384]{1,0:T(8,128)(2,1)}, s32[4,2048]{1,0:T(4,128)}, f32[4,2048]{1,0:T(4,128)}) custom-call(bf16[32,8192]{1,0:T(8,128)(2,1)} %coarse.1, bf16[32,16384]{1,0:T(8,128)(2,1)} %fine.1, s32[4,16384]{1,0:T(4,128)} %parents.1, f32[4,16384]{1,0:T(4,128)} %weights.1, bf16[256,256]{1,0:T(8,128)(2,1)} %w_parent.1, bf16[256,256]{1,0:T(8,128)(2,1)} %w_fine.1, ...), custom_call_target="tpu_custom_call" | custom-call | tf_op jit(solution)/shard_map/pallas_call | solution.py:364
  166.4 0.0 copy-done
  166.4 2.4 %broadcast_select_fusion = bf16[32,16384]{1,0:T(8,128)(2,1)} fusion(bf16[32,16384]{1,0:T(8,128)(2,1)} %get-tuple-element.6, bf16[32,16384]{1,0:T(8,128)(2,1)S(1)} %copy-done, pred[16384]{0:T(1024)(128)(4,1)S(1)} %iota_compare_fusion), kind=kLoop, calls=%fused_computation | loop fusion | flops 524288 | bytes 3162112 | tf_op jit(solution)/shard_map/jit(_where)/select_n | solution.py:395
  (1 shorter events, 0.0 us)
Async XLA Ops:
  0.7 165.7 %copy-start = (bf16[32,16384]{1,0:T(8,128)(2,1)S(1)}, bf16[32,16384]{1,0:T(8,128)(2,1)}, u32[]{:S(2)}) copy-start(bf16[32,16384]{1,0:T(8,128)(2,1)} %fine.1) | copy-start | bytes 3145732
